TPU v7x, 32 devices: a whole 2x2x4 slice. The times are simulated.
32 devices in a mesh: gx: 4 (over y, x), gy: 2 (over core), gz: 4 (over z).
Axes of the slice: x: 2, y: 2, z: 4, core: 2. Of those that a mesh axis runs over, the one named last changes fastest.
Arguments:
- panel: float32 [4, 2, 16, 256, 256], P('gx', 'gy', 'gz'), may hold values from -120 to 120
- tiles: float32 [4, 2, 16, 10, 256, 256], P('gx', 'gy', 'gz'), may hold values from -0.125 to 0.125
- codes: int32 [4, 2, 16, 10], P('gx', 'gy', 'gz'), may hold values from 0 to 26, as said below
Outputs:
- bands: float32 [4, 2, 16, 256, 256], P('gx', 'gy', 'gz')
- factor: float32 [256, 256], replicated
Inputs may be any that keep to these rules, and one draw needn't show every extreme that they name: Slot 0 of every element holds 13, the element itself; the other 9 slots of an element hold distinct codes other than 13.
All inputs are finite; a program needn't handle non-finite values.
Results may differ from a plain program's by a relative error of at most 0.0003.
Values sent between devices are 32-bit elements; how exact they have to be, the bound alone decides.
A program may use at most 128 MiB of HBM per device.

v0:
```python
import jax
import jax.numpy as jnp
from jax import lax
from jax.sharding import PartitionSpec as P


def padded_2(shard, sides, width):
    for axis, dim in sides:
        peers, length = (lax.axis_size(axis), shard.shape[dim])
        up = [(i, (i + 1) % peers) for i in range(peers - 1)]
        down = [(j, i) for i, j in up]
        last = lax.slice_in_dim(shard, length - width, length, axis=dim)
        initial = lax.slice_in_dim(shard, 0, width, axis=dim)
        before = lax.ppermute(last, axis, up)
        after = lax.ppermute(initial, axis, down)
        shard = jnp.concatenate([before, shard, after], axis=dim)
    return shard


def window(padded, first, second, third):
    zero = jnp.zeros((), jnp.int32)
    piece = lax.dynamic_slice(
        padded, (first, second, third, zero, zero), (1, 1, 1, padded.shape[3], padded.shape[4])
    )
    return piece[0, 0, 0]


def per_device(panel, tiles, codes):
    along_x = padded_2(panel, (("gx", 0),), 1)
    along_y = padded_2(along_x, (("gy", 1),), 1)
    padded = padded_2(along_y, (("gz", 2),), 1)
    width = panel.shape[4]
    products = []
    for element_cell in range(panel.shape[2]):
        slot_codes = codes[0, 0, element_cell]
        windows = jax.vmap(lambda c: window(padded, c // 9, c // 3 % 3, element_cell + c % 3))(
            slot_codes
        )
        applied = jnp.einsum(
            "kab,kbc->ac", tiles[0, 0, element_cell], windows, precision=lax.Precision.HIGHEST
        )
        products.append(applied - 0.5 * panel[0, 0, element_cell])
    filtered = jnp.stack(products)
    flat_rows = filtered.reshape(-1, width)
    local_gram = jnp.dot(flat_rows.T, flat_rows, precision=lax.Precision.HIGHEST)
    row_total = flat_rows.shape[0] * lax.axis_size("gx") * lax.axis_size("gy") * lax.axis_size("gz")
    gram_part = lax.psum_scatter(local_gram, "gz", scatter_dimension=0, tiled=True)
    gram_part = lax.psum(gram_part, ("gx", "gy"))
    summed = lax.all_gather(gram_part, "gz", axis=0, tiled=True)
    gram = summed / row_total
    lower = jnp.linalg.cholesky(gram)
    inverse = lax.linalg.triangular_solve(
        lower, jnp.eye(width, dtype=gram.dtype), left_side=True, lower=True
    )
    bands = jnp.dot(flat_rows, inverse.T, precision=lax.Precision.HIGHEST).reshape(panel.shape)
    return (bands, lower.T)


def solution(mesh):
    in_specs = (
        P("gx", "gy", "gz", None, None),
        P("gx", "gy", "gz", None, None, None),
        P("gx", "gy", "gz", None),
    )
    out_specs = (P("gx", "gy", "gz", None, None), P())
    return jax.shard_map(
        per_device, mesh=mesh, in_specs=in_specs, out_specs=out_specs, check_vma=False
    )
```

profile of v0, /device:TPU:0, one launch (start us, length us, event | category | flops | bytes accessed | tf_op | source)
XLA Modules:
  0.0 357.0 jit_solution(12483435723269355721)
XLA Ops:
  7.2 0.0 reduce-scatter.4.cloned.1.call-start
  7.2 5.1 %collective-permute-start = (f32[1,1,4,256,256]{4,3,2,1,0:T(8,128)}, f32[1,1,4,256,256]{4,3,2,1,0:T(8,128)S(1)}, u32[]{:S(2)}, u32[]{:S(2)}) collective-permute-start(f32[1,1,4,256,256]{4,3,2,1,0:T(8,128)} %param.3), channel_id=1, source_target_pairs={{0,8},{8,16},{16,24},{1,9},{9,17},{17,25},{2,10},{10,18},{18,26},{... | collective-permute-start | bytes 3145736 | tf_op jit(solution)/shard_map/ppermute | solution.py:14
  12.3 1.3 collective-permute-start.1
  13.6 21.3 %collective-permute-done = f32[1,1,4,256,256]{4,3,2,1,0:T(8,128)S(1)} collective-permute-done((f32[1,1,4,256,256]{4,3,2,1,0:T(8,128)}, f32[1,1,4,256,256]{4,3,2,1,0:T(8,128)S(1)}, u32[]{:S(2)}, u32[]{:S(2)}) %collective-permute-start) | collective-permute-done | bytes 1048608 | tf_op jit(solution)/shard_map/ppermute | solution.py:14
  34.9 0.1 constant_dynamic-update-slice_fusion.2
  35.0 0.1 constant_dynamic-update-slice_fusion.1
  35.1 24.1 %collective-permute-done.1 = f32[1,1,4,256,256]{4,3,2,1,0:T(8,128)S(1)} collective-permute-done((f32[1,1,4,256,256]{4,3,2,1,0:T(8,128)}, f32[1,1,4,256,256]{4,3,2,1,0:T(8,128)S(1)}, u32[]{:S(2)}, u32[]{:S(2)}) %collective-permute-start.1) | collective-permute-done | bytes 1048608 | tf_op jit(solution)/shard_map/ppermute | solution.py:15
  59.3 0.1 constant_dynamic-update-slice_fusion
  59.3 1.5 collective-permute-start.2
  60.8 1.3 collective-permute-start.3
  62.1 3.8 %collective-permute-done.2 = f32[3,1,4,256,256]{4,3,2,1,0:T(8,128)S(1)} collective-permute-done((f32[3,1,4,256,256]{4,3,2,1,0:T(8,128)S(1)}, f32[3,1,4,256,256]{4,3,2,1,0:T(8,128)S(1)}, u32[]{:S(2)}, u32[]{:S(2)}) %collective-permute-start.2) | collective-permute-done | bytes 3145760 | tf_op jit(solution)/shard_map/ppermute | solution.py:14
  65.9 2.5 collective-permute-done.3
  68.4 2.8 pad_maximum_fusion.3
  71.2 0.2 copy-done.1
  71.4 5.0 %collective-permute-start.4 = (f32[3,3,1,256,256]{4,3,2,1,0:T(8,128)}, f32[3,3,1,256,256]{4,3,2,1,0:T(8,128)}, u32[]{:S(2)}, u32[]{:S(2)}) collective-permute-start(f32[3,3,1,256,256]{4,3,2,1,0:T(8,128)} %get-tuple-element.24), channel_id=1, source_target_pairs={{0,1},{1,2},{2,3},{4,5},{5,6},{6,7},{8,9},{9,10},{10,11},{12,13},{... | collective-permute-start | bytes 7077896 | tf_op jit(solution)/shard_map/ppermute | solution.py:14
  76.4 1.3 collective-permute-start.5
  77.7 0.9 fusion.104
  78.6 0.9 copy.46
  79.5 1.1 copy.45
  80.6 1.8 copy.44
  82.4 1.8 copy.43
  84.2 0.1 fusion.100
  84.2 41.9 %collective-permute-done.4 = f32[3,3,1,256,256]{4,3,2,1,0:T(8,128)} collective-permute-done((f32[3,3,1,256,256]{4,3,2,1,0:T(8,128)}, f32[3,3,1,256,256]{4,3,2,1,0:T(8,128)}, u32[]{:S(2)}, u32[]{:S(2)}) %collective-permute-start.4) | collective-permute-done | bytes 2359328 | tf_op jit(solution)/shard_map/ppermute | solution.py:14
  126.1 5.5 %collective-permute-done.5 = f32[3,3,1,256,256]{4,3,2,1,0:T(8,128)} collective-permute-done((f32[3,3,1,256,256]{4,3,2,1,0:T(8,128)}, f32[3,3,1,256,256]{4,3,2,1,0:T(8,128)}, u32[]{:S(2)}, u32[]{:S(2)}) %collective-permute-start.5) | collective-permute-done | bytes 2359328 | tf_op jit(solution)/shard_map/ppermute | solution.py:15
  131.7 9.9 %pad_maximum_fusion = f32[3,3,6,256,256]{4,3,2,1,0:T(8,128)} fusion(f32[3,3,1,256,256]{4,3,2,1,0:T(8,128)} %collective-permute-done.5, f32[3,1,4,256,256]{4,3,2,1,0:T(8,128)} %copy-done.1, f32[3,1,4,256,256]{4,3,2,1,0:T(8,128)S(1)} %constant_dynamic-update-slice_fusion, f32[3,1,4,256,256]{4,3,2,1,0:T(8,128)} %copy-done, ...), kind=kLoop, calls=%fused_computation.6 | loop fusion | flops 14155776 | bytes 28311552 | tf_op jit(solution)/shard_map/concatenate | solution.py:16
  141.6 7.3 %gather_fusion.3 = f32[10,256,256]{2,1,0:T(8,128)} fusion(f32[3,3,6,256,256]{4,3,2,1,0:T(8,128)} %pad_maximum_fusion, s32[10]{0:T(128)S(1)} %get-tuple-element.38), kind=kCustom, calls=%fused_computation.3 | custom fusion | bytes 5243080 | tf_op jit(solution)/shard_map/vmap()/gather | solution.py:22
  148.9 7.4 %gather_fusion.2 = f32[10,256,256]{2,1,0:T(8,128)} fusion(f32[3,3,6,256,256]{4,3,2,1,0:T(8,128)} %pad_maximum_fusion, s32[10]{0:T(128)S(1)} %get-tuple-element.39), kind=kCustom, calls=%fused_computation.2 | custom fusion | bytes 5243080 | tf_op jit(solution)/shard_map/vmap()/gather | solution.py:22
  156.2 5.7 %gather_fusion.1 = f32[10,256,256]{2,1,0:T(8,128)S(1)} fusion(f32[3,3,6,256,256]{4,3,2,1,0:T(8,128)} %pad_maximum_fusion, s32[10]{0:T(128)S(1)} %get-tuple-element.37), kind=kCustom, calls=%fused_computation.1 | custom fusion | bytes 5243080 | tf_op jit(solution)/shard_map/vmap()/gather | solution.py:22
  162.0 7.4 %gather_fusion = f32[10,256,256]{2,1,0:T(8,128)} fusion(f32[3,3,6,256,256]{4,3,2,1,0:T(8,128)} %pad_maximum_fusion, s32[10]{0:T(128)S(1)} %get-tuple-element.36), kind=kCustom, calls=%fused_computation | custom fusion | bytes 5243080 | tf_op jit(solution)/shard_map/vmap()/gather | solution.py:22
  169.4 0.0 copy-done.7
  169.4 7.0 %fusion.27 = f32[1,256,256]{1,2,0:T(8,128)S(1)} fusion(f32[10,256,256]{2,1,0:T(8,128)} %gather_fusion.3, f32[1,1,4,10,256,256]{5,4,3,2,1,0:T(8,128)} %param.4, f32[1,1,1,256,256]{3,4,2,1,0:T(8,128)S(1)} %copy-done.7), kind=kOutput, calls=%fused_computation.29 | convolution fusion | flops 2013396992 | bytes 5767168 | tf_op jit(solution)/shard_map/kab,kbc->ac/dot_general | solution.py:39
  176.4 0.0 copy-start.5
  176.4 6.2 %fusion.33 = f32[1,256,256]{1,2,0:T(8,128)S(1)} fusion(f32[10,256,256]{2,1,0:T(8,128)S(1)} %copy-done.3, f32[1,1,4,10,256,256]{5,4,3,2,1,0:T(8,128)} %param.4, f32[1,1,1,256,256]{3,4,2,1,0:T(8,128)S(1)} %copy.45), kind=kOutput, calls=%fused_computation.31 | convolution fusion | flops 2013396992 | bytes 5767168 | tf_op jit(solution)/shard_map/kab,kbc->ac/dot_general | solution.py:39
  182.7 6.3 %fusion.39 = f32[1,256,256]{1,2,0:T(8,128)S(1)} fusion(f32[10,256,256]{2,1,0:T(8,128)S(1)} %gather_fusion.1, f32[1,1,4,10,256,256]{5,4,3,2,1,0:T(8,128)} %param.4, f32[1,1,1,256,256]{3,4,2,1,0:T(8,128)S(1)} %copy-done.5), kind=kOutput, calls=%fused_computation.33 | convolution fusion | flops 2013396992 | bytes 5767168 | tf_op jit(solution)/shard_map/kab,kbc->ac/dot_general | solution.py:39
  189.0 6.2 %fusion.45 = f32[1,256,256]{1,2,0:T(8,128)S(1)} fusion(f32[10,256,256]{2,1,0:T(8,128)S(1)} %copy-done.2, f32[1,1,4,10,256,256]{5,4,3,2,1,0:T(8,128)} %param.4, f32[1,1,1,256,256]{3,4,2,1,0:T(8,128)S(1)} %copy-done.6), kind=kOutput, calls=%fused_computation.35 | convolution fusion | flops 2013396992 | bytes 5767168 | tf_op jit(solution)/shard_map/kab,kbc->ac/dot_general | solution.py:39
  195.2 1.7 convolution_bitcast_fusion.1
  197.0 0.0 reduce-scatter.4.cloned.1.call-update
  197.0 0.0 all-reduce.3.cloned.1.call-start
  197.1 18.0 %reduce-scatter.4.cloned.1.call-done = f32[64,256]{1,0:T(8,128)} async-done(((f32[256,256]{1,0:T(8,128)}), f32[64,256]{1,0:T(8,128)}) %reduce-scatter.4.cloned.1.call-update) | async-done | bytes 65552
  215.0 1.6 copy.42
  216.6 0.0 all-reduce.3.cloned.1.call-update
  216.7 53.7 %all-reduce.3.cloned.1.call-done = f32[64,256]{0,1:T(8,128)} async-done(((f32[64,256]{0,1:T(8,128)}), f32[64,256]{0,1:T(8,128)}) %all-reduce.3.cloned.1.call-update) | async-done | bytes 65552 | tf_op jit(solution)/shard_map/psum | solution.py:48
  270.4 1.0 copy.28
  271.3 14.1 %all_gather.3 = f32[256,256]{1,0:T(8,128)S(1)} all-gather(f32[64,256]{1,0:T(8,128)S(1)} %copy.28), channel_id=1, replica_groups=mesh['gx'=4,'gy'=2,'gz'=4] {'gz'}, dimensions={0}, use_global_device_ids=true | all-gather | bytes 327680 | tf_op jit(solution)/shard_map/all_gather | solution.py:49
  285.5 0.1 copy.29
  285.6 0.1 copy.30
  285.8 11.7 %cholesky.50 = f32[128,128]{1,0:T(8,128)S(1)} custom-call(f32[128,128]{1,0:T(8,128)S(1)} %cholesky.118), custom_call_target="Cholesky" | custom-call | tf_op jit(solution)/shard_map/jit(cholesky)/cholesky | solution.py:51
  297.6 9.8 %custom-call.14 = f32[1,128,128]{1,2,0:T(8,128)S(1)} custom-call(f32[1,128,128]{2,1,0:T(8,128)S(1)} %get-tuple-element.35), custom_call_target="InvertDiagBlocksLowerTriangular" | custom-call | tf_op jit(solution)/shard_map/jit(cholesky)/cholesky | solution.py:51
  307.4 0.2 constant_dynamic-update-slice_fusion.4
  307.6 0.3 convolution_subtract_fusion.1
  307.9 11.7 %cholesky.105 = f32[128,128]{1,0:T(8,128)S(1)} custom-call(f32[128,128]{1,0:T(8,128)S(1)} %convolution_subtract_fusion.1), custom_call_target="Cholesky" | custom-call | tf_op jit(solution)/shard_map/jit(cholesky)/cholesky | solution.py:51
  319.7 0.6 compare_reduce_fusion
  321.6 0.1 triangular_solve.63
  321.6 4.1 %while.1 = (s32[]{:T(128)}, f32[256,256]{1,0:T(8,128)S(1)}, s32[2,2]{1,0:T(2,128)S(1)}, f32[2,128,128]{2,1,0:T(8,128)S(1)}, s32[]{:T(128)}) while((s32[]{:T(128)}, f32[256,256]{1,0:T(8,128)S(1)}, s32[2,2]{1,0:T(2,128)S(1)}, f32[2,128,128]{2,1,0:T(8,128)S(1)}, s32[]{:T(128)}) %tuple.37), condition=%wide.while_cond, body=%wide.while_body.sunk | while | flops 2 | bytes 131181 | solution.py:52
  321.9 0.6 fusion.114
  322.5 1.3 bitcast_dynamic-update-slice_fusion.2
  323.8 0.6 fusion.114
  324.4 1.3 bitcast_dynamic-update-slice_fusion.2
  325.7 19.7 %custom-call.15 = f32[2,128,128]{1,2,0:T(8,128)S(1)} custom-call(f32[2,128,128]{2,1,0:T(8,128)S(1)} %get-tuple-element.9), custom_call_target="InvertDiagBlocksLowerTriangular" | custom-call | tf_op jit(solution)/shard_map/triangular_solve | solution.py:52
  345.4 0.3 fusion.53
  345.7 0.3 convolution_subtract_fusion
  345.9 0.3 fusion.56
  346.2 2.8 convolution_bitcast_fusion
  349.0 0.8 copy.32
  (27 shorter events, 0.3 us)
Async XLA Ops:
  7.2 207.9 %reduce-scatter.4.cloned.1.call-start = ((), (), s32[]{:S(2)}) async-start(), calls=%async_computation.2 | async-start | bytes 327680
  7.2 27.8 %copy-start.4 = (f32[1,1,4,256,256]{4,3,2,1,0:T(8,128)S(1)}, f32[1,1,4,256,256]{4,3,2,1,0:T(8,128)}, u32[]{:S(2)}) copy-start(f32[1,1,4,256,256]{4,3,2,1,0:T(8,128)} %param.3) | copy-start | bytes 3145732
  7.2 27.7 %collective-permute-start = (f32[1,1,4,256,256]{4,3,2,1,0:T(8,128)}, f32[1,1,4,256,256]{4,3,2,1,0:T(8,128)S(1)}, u32[]{:S(2)}, u32[]{:S(2)}) collective-permute-start(f32[1,1,4,256,256]{4,3,2,1,0:T(8,128)} %param.3), channel_id=1, source_target_pairs={{0,8},{8,16},{16,24},{1,9},{9,17},{17,25},{2,10},{10,18},{18,26},{... | collective-permute-start | bytes 3145736 | tf_op jit(solution)/shard_map/ppermute | solution.py:14
  12.3 47.0 %collective-permute-start.1 = (f32[1,1,4,256,256]{4,3,2,1,0:T(8,128)}, f32[1,1,4,256,256]{4,3,2,1,0:T(8,128)S(1)}, u32[]{:S(2)}, u32[]{:S(2)}) collective-permute-start(f32[1,1,4,256,256]{4,3,2,1,0:T(8,128)} %param.3), channel_id=1, source_target_pairs={{8,0},{16,8},{24,16},{9,1},{17,9},{25,17},{10,2},{18,10},{26,18},{... | collective-permute-start | bytes 3145736 | tf_op jit(solution)/shard_map/ppermute | solution.py:15
  59.3 6.6 %collective-permute-start.2 = (f32[3,1,4,256,256]{4,3,2,1,0:T(8,128)S(1)}, f32[3,1,4,256,256]{4,3,2,1,0:T(8,128)S(1)}, u32[]{:S(2)}, u32[]{:S(2)}) collective-permute-start(f32[3,1,4,256,256]{4,3,2,1,0:T(8,128)S(1)} %constant_dynamic-update-slice_fusion), channel_id=1, source_target_pairs={{0,4},{1,5},{2,6},{3,7},{8,12},{9,13},{10,14},{11,15},{16,20},{17,... | collective-permute-start | bytes 9437192 | tf_op jit(solution)/shard_map/ppermute | solution.py:14
  60.8 7.6 %collective-permute-start.3 = (f32[3,1,4,256,256]{4,3,2,1,0:T(8,128)S(1)}, f32[3,1,4,256,256]{4,3,2,1,0:T(8,128)S(1)}, u32[]{:S(2)}, u32[]{:S(2)}) collective-permute-start(f32[3,1,4,256,256]{4,3,2,1,0:T(8,128)S(1)} %constant_dynamic-update-slice_fusion), channel_id=1, source_target_pairs={{4,0},{5,1},{6,2},{7,3},{12,8},{13,9},{14,10},{15,11},{20,16},{21,... | collective-permute-start | bytes 9437192 | tf_op jit(solution)/shard_map/ppermute | solution.py:15
  65.9 5.3 %copy-start = (f32[3,1,4,256,256]{4,3,2,1,0:T(8,128)}, f32[3,1,4,256,256]{4,3,2,1,0:T(8,128)S(1)}, u32[]{:S(2)}) copy-start(f32[3,1,4,256,256]{4,3,2,1,0:T(8,128)S(1)} %collective-permute-done.2) | copy-start | bytes 9437188
  68.4 3.0 copy-start.1
  71.4 12.8 %copy-start.8 = (s32[1,1,4,10]{3,2,1,0:T(4,128)S(1)}, s32[1,1,4,10]{3,2,1,0:T(4,128)}, u32[]{:S(2)}) copy-start(s32[1,1,4,10]{3,2,1,0:T(4,128)} %param.5) | copy-start | bytes 484
  71.4 54.7 %collective-permute-start.4 = (f32[3,3,1,256,256]{4,3,2,1,0:T(8,128)}, f32[3,3,1,256,256]{4,3,2,1,0:T(8,128)}, u32[]{:S(2)}, u32[]{:S(2)}) collective-permute-start(f32[3,3,1,256,256]{4,3,2,1,0:T(8,128)} %get-tuple-element.24), channel_id=1, source_target_pairs={{0,1},{1,2},{2,3},{4,5},{5,6},{6,7},{8,9},{9,10},{10,11},{12,13},{... | collective-permute-start | bytes 7077896 | tf_op jit(solution)/shard_map/ppermute | solution.py:14
  76.4 55.2 %collective-permute-start.5 = (f32[3,3,1,256,256]{4,3,2,1,0:T(8,128)}, f32[3,3,1,256,256]{4,3,2,1,0:T(8,128)}, u32[]{:S(2)}, u32[]{:S(2)}) collective-permute-start(f32[3,3,1,256,256]{4,3,2,1,0:T(8,128)} %get-tuple-element.25), channel_id=1, source_target_pairs={{1,0},{2,1},{3,2},{5,4},{6,5},{7,6},{9,8},{10,9},{11,10},{13,12},{... | collective-permute-start | bytes 7077896 | tf_op jit(solution)/shard_map/ppermute | solution.py:15
  162.0 7.4 %copy-start.7 = (f32[1,1,1,256,256]{3,4,2,1,0:T(8,128)S(1)}, f32[1,1,1,256,256]{3,4,2,1,0:T(8,128)}, u32[]{:S(2)}) copy-start(f32[1,1,1,256,256]{3,4,2,1,0:T(8,128)} %copy.46) | copy-start | bytes 786436
  169.4 7.0 %copy-start.3 = (f32[10,256,256]{2,1,0:T(8,128)S(1)}, f32[10,256,256]{2,1,0:T(8,128)}, u32[]{:S(2)}) copy-start(f32[10,256,256]{2,1,0:T(8,128)} %gather_fusion.2) | copy-start | bytes 7864324
  176.4 6.3 %copy-start.5 = (f32[1,1,1,256,256]{3,4,2,1,0:T(8,128)S(1)}, f32[1,1,1,256,256]{3,4,2,1,0:T(8,128)}, u32[]{:S(2)}) copy-start(f32[1,1,1,256,256]{3,4,2,1,0:T(8,128)} %copy.44) | copy-start | bytes 786436
  182.6 6.4 %copy-start.2 = (f32[10,256,256]{2,1,0:T(8,128)S(1)}, f32[10,256,256]{2,1,0:T(8,128)}, u32[]{:S(2)}) copy-start(f32[10,256,256]{2,1,0:T(8,128)} %gather_fusion) | copy-start | bytes 7864324
  182.7 6.4 %copy-start.6 = (f32[1,1,1,256,256]{3,4,2,1,0:T(8,128)S(1)}, f32[1,1,1,256,256]{3,4,2,1,0:T(8,128)}, u32[]{:S(2)}) copy-start(f32[1,1,1,256,256]{3,4,2,1,0:T(8,128)} %copy.43) | copy-start | bytes 786436
  197.0 73.4 %all-reduce.3.cloned.1.call-start = ((), (), s32[]{:S(2)}) async-start(), calls=%async_computation.1 | async-start | bytes 262144 | tf_op jit(solution)/shard_map/psum | solution.py:48
Sparse Core Ops, SparseCore 0:
  197.1 17.8 reduce-scatter.3
  218.6 51.6 all-reduce.2
where the time goes:
time: 360 us; the launch traced here: 357 us
  waiting for transfers between devices  171 us (48%)
  other arithmetic  66.5 us (18%)
  local copies, waits for them, and re-layouts  42.3 us (12%)
  matrix products  31.6 us (9%)
  between operations  15.9 us (4%)
  starting transfers between devices  15.5 us (4%)
  blocking collectives  14.1 us (4%)
    ppermute x3, waiting for transfers between devices, padded_2(): before = lax.ppermute(last, axis, up)  67 us
    psum x1, waiting for transfers between devices, per_device(): gram_part = lax.psum(gram_part, ('gx', 'gy'))  53.7 us
    another operation x6, other arithmetic, per_device(): lower = jnp.linalg.cholesky(gram)  34 us
    ppermute x3, waiting for transfers between devices, padded_2(): after = lax.ppermute(initial, axis, down)  32.1 us
    gather x4, local copies, waits for them, and re-layouts, window(): lax.dynamic_slice(padded, (first, second, third, zero, zero), (1, 1, 1, p...  27.8 us
    dot_general x4, matrix products, per_device(): jnp.einsum('kab,kbc->ac', tiles[0, 0, element_cell], windows, precision=l...  25.7 us
    another operation x2, other arithmetic, per_device(): lax.linalg.triangular_solve(lower, jnp.eye(width, dtype=gram.dtype), left...  19.7 us
    unnamed x3, waiting for transfers between devices  18 us
  transfers between devices with their start and end apart: 8, of which 8 were waited for; matrix products, arithmetic and copies ran while one was open for 2% of the time, Pallas kernels for 0%

commit v1 on v0

v1 whole, which is shorter than its diff:
```python
import functools
import jax
import jax.numpy as jnp
from jax import lax
from jax.experimental import pallas as pl
from jax.experimental.pallas import tpu as pltpu
from jax.sharding import PartitionSpec as P

MESH = pl.DeviceIdType.MESH
PIECES = 2
BLOCK = 32


def split(value):
    high = value.astype(jnp.bfloat16)
    low = (value - high.astype(jnp.float32)).astype(jnp.bfloat16)
    return high, low


def product(left, right, dims):
    dot = functools.partial(
        lax.dot_general, dimension_numbers=(dims, ((), ())), preferred_element_type=jnp.float32
    )
    return dot(left[0], right[0]) + (dot(left[0], right[1]) + dot(left[1], right[0]))


def halo_kernel(sizes, panel_ref, halo_ref, x_sent, z_sent, y_sent, arrived):
    nx, ny, nz = sizes
    ix, iy, iz = (lax.axis_index(a) for a in ("gx", "gy", "gz"))
    depth, rows = panel_ref.shape[2], panel_ref.shape[3]
    part = rows // PIECES
    squared = nx == 4
    below, above = iz > 0, iz < nz - 1
    front, back = iy > 0, iy < ny - 1

    if squared:
        across = ix + 1 - 2 * lax.rem(ix, 2)
        beside = lax.rem(ix + 2, 4)
        slot_a, valid_a = 2 * lax.rem(ix + 1, 2), None
        slot_b, valid_b = 2 - slot_a, (ix == 1) | (ix == 2)
        relays = (ix == 0) | (ix == 3)
        partners_x = ((across, None), (beside, None))
    else:
        slot_a, valid_a = jnp.int32(0), ix > 0
        slot_b, valid_b = jnp.int32(2), ix < nx - 1
        partners_x = ((ix - 1, valid_a), (ix + 1, valid_b))

    def when(cond, action):
        if cond is None:
            action()
        else:
            pl.when(cond)(action)

    def both(*conds):
        conds = [c for c in conds if c is not None]
        return functools.reduce(jnp.logical_and, conds) if conds else None

    barrier = pltpu.get_barrier_semaphore()
    partners = (
        [("gx", d, c) for d, c in partners_x]
        + [("gz", iz - 1, below), ("gz", iz + 1, above)]
        + [("gy", iy - 1, front), ("gy", iy + 1, back)]
    )
    total = jnp.int32(0)
    for axis, device, cond in partners:
        when(
            cond,
            lambda axis=axis, device=device: pl.semaphore_signal(
                barrier, inc=1, device_id={axis: device}, device_id_type=MESH
            ),
        )
        total = total + (1 if cond is None else cond.astype(jnp.int32))
    pl.semaphore_wait(barrier, total)

    sends = []

    def own(z, c):
        return panel_ref.at[0, 0, z, pl.ds(c * part, part)]

    def cell(a, b, z, c):
        return halo_ref.at[a, b, z, pl.ds(c * part, part)]

    def send(cond, source, target, sem, slot, axis, device):
        a, b, z, c = slot

        def start():
            pltpu.make_async_remote_copy(
                src_ref=source,
                dst_ref=target,
                send_sem=sem,
                recv_sem=arrived.at[a, b, z, c],
                device_id={axis: device},
                device_id_type=MESH,
            ).start()

        when(cond, start)
        sends.append((cond, source, sem))

    def wait(cond, a, b, z, c):
        ref = cell(a, b, z, c)
        when(cond, lambda: pltpu.make_async_copy(ref, ref, arrived.at[a, b, z, c]).wait())

    def send_y(cond, source, a, z, c):
        send(both(cond, front), source, cell(a, 2, z, c), y_sent.at[0, a, z, c],
             (a, 2, z, c), "gy", iy - 1)
        send(both(cond, back), source, cell(a, 0, z, c), y_sent.at[1, a, z, c],
             (a, 0, z, c), "gy", iy + 1)

    def send_z(cond, source, a, z, c):
        if z == 0:
            send(both(cond, below), source, cell(a, 1, depth + 1, c), z_sent.at[0, a, c],
                 (a, 1, depth + 1, c), "gz", iz - 1)
        if z == depth - 1:
            send(both(cond, above), source, cell(a, 1, 0, c), z_sent.at[1, a, c],
                 (a, 1, 0, c), "gz", iz + 1)

    order = [0, depth - 1] + list(range(1, depth - 1)) if depth > 1 else [0]
    for z in order:
        for c in range(PIECES):
            if squared:
                target = 2 * lax.rem(ix, 2)
                send(None, own(z, c), cell(target, 1, z + 1, c), x_sent.at[0, z, c],
                     (target, 1, z + 1, c), "gx", across)
            else:
                send(valid_a, own(z, c), cell(2, 1, z + 1, c), x_sent.at[0, z, c],
                     (2, 1, z + 1, c), "gx", ix - 1)
                send(valid_b, own(z, c), cell(0, 1, z + 1, c), x_sent.at[1, z, c],
                     (0, 1, z + 1, c), "gx", ix + 1)
            send_z(None, own(z, c), 1, z, c)
    for z in order:
        for c in range(PIECES):
            send_y(None, own(z, c), 1, z + 1, c)

    def arrive(cond, a, z, c, relay=False):
        wait(cond, a, 1, z + 1, c)
        if relay and squared:
            target = 2 - a
            send(relays, cell(a, 1, z + 1, c), cell(target, 1, z + 1, c), x_sent.at[1, z, c],
                 (target, 1, z + 1, c), "gx", beside)
        send_z(cond, cell(a, 1, z + 1, c), a, z, c)
        send_y(cond, cell(a, 1, z + 1, c), a, z + 1, c)

    def arrive_z(cond, a):
        for side, slot in ((below, 0), (above, depth + 1)):
            for c in range(PIECES):
                ok = both(cond, side)
                wait(ok, a, 1, slot, c)
                send_y(ok, cell(a, 1, slot, c), a, slot, c)

    steps = [(k, c) for k in order for c in range(PIECES)]
    for at in range(len(steps) + 1):
        if at < len(steps):
            arrive(valid_a, slot_a, *steps[at], relay=True)
        if at >= 1:
            arrive(valid_b, slot_b, *steps[at - 1])
        if at == len(steps) // 2:
            arrive_z(None, 1)
        if at == len(steps) - 1:
            arrive_z(valid_a, slot_a)
    arrive_z(valid_b, slot_b)

    for b, side in ((0, front), (2, back)):
        for a, cond in ((1, None), (slot_a, valid_a), (slot_b, valid_b)):
            for z in range(depth + 2):
                edge = below if z == 0 else above if z == depth + 1 else None
                for c in range(PIECES):
                    wait(both(cond, edge, side), a, b, z, c)
    for cond, source, sem in sends:
        when(cond, lambda source=source, sem=sem: pltpu.make_async_copy(source, source, sem).wait())


def exchange_halo(panel, sizes):
    depth, rows, width = panel.shape[2:]
    return pl.pallas_call(
        functools.partial(halo_kernel, sizes),
        out_shape=jax.ShapeDtypeStruct((3, 3, depth + 2, rows, width), panel.dtype),
        in_specs=[pl.BlockSpec(memory_space=pl.ANY)],
        out_specs=pl.BlockSpec(memory_space=pl.ANY),
        scratch_shapes=[
            pltpu.SemaphoreType.DMA((2, depth, PIECES)),
            pltpu.SemaphoreType.DMA((2, 3, PIECES)),
            pltpu.SemaphoreType.DMA((2, 3, depth + 2, PIECES)),
            pltpu.SemaphoreType.DMA((3, 3, depth + 2, PIECES)),
        ],
        compiler_params=pltpu.CompilerParams(collective_id=0, has_side_effects=True),
        name="halo",
    )(panel)


def filter_kernel(sizes, codes_ref, panel_ref, tiles_ref, halo_ref, rows_ref, gram_ref,
                  tile_buf, window_buf, own_buf, tile_sem, window_sem, own_sem):
    nx, ny, nz = sizes
    ix, iy, iz = (lax.axis_index(a) for a in ("gx", "gy", "gz"))
    depth, slots = tiles_ref.shape[2], tiles_ref.shape[3]
    own = pltpu.make_async_copy(panel_ref.at[0, 0], own_buf, own_sem)
    own.start()

    def place(e, s):
        code = codes_ref[0, 0, e, s]
        a = code // 9
        b = lax.rem(code // 3, 3)
        z = e + lax.rem(code, 3)
        x_at, y_at, z_at = ix + a - 1, iy + b - 1, iz * depth + z - 1
        inside = ((x_at >= 0) & (x_at < nx) & (y_at >= 0) & (y_at < ny)
                  & (z_at >= 0) & (z_at < nz * depth))
        local = (a == 1) & (b == 1) & (z >= 1) & (z <= depth)
        return a, b, z, inside, local

    for e in range(depth):
        pltpu.make_async_copy(tiles_ref.at[0, 0, e], tile_buf.at[e], tile_sem.at[e]).start()

        def fetch(s, carry, e=e):
            a, b, z, inside, local = place(e, s)
            target, sem = window_buf.at[e, s], window_sem.at[e, s]

            @pl.when(inside & local)
            def _():
                pltpu.make_async_copy(panel_ref.at[0, 0, z - 1], target, sem).start()

            @pl.when(inside & jnp.logical_not(local))
            def _():
                pltpu.make_async_copy(halo_ref.at[a, b, z], target, sem).start()

            @pl.when(jnp.logical_not(inside))
            def _():
                window_buf[e, s] = jnp.zeros(window_buf.shape[2:], window_buf.dtype)

            return carry

        lax.fori_loop(0, slots, fetch, 0)
    own.wait()
    for e in range(depth):
        pltpu.make_async_copy(tiles_ref.at[0, 0, e], tile_buf.at[e], tile_sem.at[e]).wait()

        def apply(s, total, e=e):
            inside = place(e, s)[3]

            @pl.when(inside)
            def _():
                pltpu.make_async_copy(
                    window_buf.at[e, s], window_buf.at[e, s], window_sem.at[e, s]
                ).wait()

            return total + product(
                split(tile_buf[e, s]), split(window_buf[e, s]), ((1,), (0,))
            )

        filtered = lax.fori_loop(0, slots, apply, -0.5 * own_buf[e], unroll=2)
        rows_ref[e] = filtered
        pieces = split(filtered)
        term = product(pieces, pieces, ((0,), (0,)))
        gram_ref[...] = term if e == 0 else gram_ref[...] + term


def apply_filter(codes, panel, tiles, halo, sizes):
    depth, slots, rows, width = tiles.shape[2], tiles.shape[3], panel.shape[3], panel.shape[4]
    hbm = pl.BlockSpec(memory_space=pl.ANY)
    vmem = pl.BlockSpec(memory_space=pltpu.VMEM)
    return pl.pallas_call(
        functools.partial(filter_kernel, sizes),
        out_shape=(
            jax.ShapeDtypeStruct((depth, rows, width), jnp.float32),
            jax.ShapeDtypeStruct((width, width), jnp.float32),
        ),
        in_specs=[pl.BlockSpec(memory_space=pltpu.SMEM), hbm, hbm, hbm],
        out_specs=(vmem, vmem),
        scratch_shapes=[
            pltpu.VMEM((depth, slots, rows, rows), jnp.float32),
            pltpu.VMEM((depth, slots, rows, width), jnp.float32),
            pltpu.VMEM((depth, rows, width), jnp.float32),
            pltpu.SemaphoreType.DMA((depth,)),
            pltpu.SemaphoreType.DMA((depth, slots)),
            pltpu.SemaphoreType.DMA,
        ],
        compiler_params=pltpu.CompilerParams(vmem_limit_bytes=48 << 20),
        name="filter",
    )(codes, panel, tiles, halo)


def sum_kernel(sizes, gram_ref, out_ref, own, from_y, part_y, from_x, from_z, full,
               local_sem, y_send, y_recv, x_send, x_recv, z_send, z_recv,
               gx_send, gx_recv, gy_send, gy_recv):
    nx, ny, nz = sizes
    ix, iy, iz = (lax.axis_index(a) for a in ("gx", "gy", "gz"))
    rows_y = gram_ref.shape[0] // ny
    rows_x = rows_y // nx
    barrier = pltpu.get_barrier_semaphore()
    peers = {
        axis: [lax.rem(at + d, n) for d in range(1, n)]
        for axis, at, n in (("gx", ix, nx), ("gy", iy, ny), ("gz", iz, nz))
    }
    for axis, group in peers.items():
        for peer in group:
            pl.semaphore_signal(barrier, inc=1, device_id={axis: peer}, device_id_type=MESH)
    pl.semaphore_wait(barrier, nx + ny + nz - 3)

    def copy(source, target, send_sem, recv_sem, axis, peer):
        remote = pltpu.make_async_remote_copy(
            src_ref=source, dst_ref=target, send_sem=send_sem, recv_sem=recv_sem,
            device_id={axis: peer}, device_id_type=MESH,
        )
        remote.start()
        return remote

    def finish(copies):
        for remote in copies:
            remote.wait()

    def block(ref, at, count):
        return ref.at[pl.ds(pl.multiple_of(at * count, count), count)]

    finish([
        copy(block(gram_ref, peer, rows_y), from_y.at[d], y_send.at[d], y_recv.at[d], "gy", peer)
        for d, peer in enumerate(peers["gy"])
    ])
    total = gram_ref[pl.ds(pl.multiple_of(iy * rows_y, rows_y), rows_y), :]
    for d in range(ny - 1):
        total = total + from_y[d]
    part_y[...] = total
    finish([
        copy(block(part_y, peer, rows_x), from_x.at[d], x_send.at[d], x_recv.at[d], "gx", peer)
        for d, peer in enumerate(peers["gx"])
    ])
    total = part_y[pl.ds(pl.multiple_of(ix * rows_x, rows_x), rows_x), :]
    for d in range(nx - 1):
        total = total + from_x[d]
    from_z[pl.ds(iz, 1)] = total[None]
    started = [
        copy(from_z.at[iz], from_z.at[iz], z_send.at[d], z_recv.at[iz], "gz", peer)
        for d, peer in enumerate(peers["gz"])
    ]
    for remote in started:
        remote.wait_send()
    for peer in peers["gz"]:
        ref = from_z.at[peer]
        pltpu.make_async_copy(ref, ref, z_recv.at[peer]).wait()
    total = from_z[0]
    for d in range(1, nz):
        total = total + from_z[d]
    mine = iy * nx + ix
    full[pl.ds(pl.multiple_of(mine * rows_x, rows_x), rows_x), :] = total
    started = [
        copy(block(full, mine, rows_x), block(full, mine, rows_x), gx_send.at[d], gx_recv.at[ix],
             "gx", peer)
        for d, peer in enumerate(peers["gx"])
    ]
    for remote in started:
        remote.wait_send()
    for peer in peers["gx"]:
        ref = block(full, iy * nx + peer, rows_x)
        pltpu.make_async_copy(ref, ref, gx_recv.at[peer]).wait()
    started = [
        copy(block(full, iy, rows_y), block(full, iy, rows_y), gy_send.at[d], gy_recv.at[iy],
             "gy", peer)
        for d, peer in enumerate(peers["gy"])
    ]
    for remote in started:
        remote.wait_send()
    for peer in peers["gy"]:
        ref = block(full, peer, rows_y)
        pltpu.make_async_copy(ref, ref, gy_recv.at[peer]).wait()
    out_ref[...] = full[...]


def sum_gram(gram, sizes):
    nx, ny, nz = sizes
    size = gram.shape[0]
    rows_y = size // ny
    rows_x = rows_y // nx
    vmem = pl.BlockSpec(memory_space=pltpu.VMEM)
    dma = pltpu.SemaphoreType.DMA
    return pl.pallas_call(
        functools.partial(sum_kernel, sizes),
        out_shape=jax.ShapeDtypeStruct(gram.shape, gram.dtype),
        in_specs=[vmem],
        out_specs=vmem,
        scratch_shapes=[
            pltpu.VMEM((8, 128), jnp.float32),
            pltpu.VMEM((max(ny - 1, 1), rows_y, size), jnp.float32),
            pltpu.VMEM((rows_y, size), jnp.float32),
            pltpu.VMEM((max(nx - 1, 1), rows_x, size), jnp.float32),
            pltpu.VMEM((nz, rows_x, size), jnp.float32),
            pltpu.VMEM((size, size), jnp.float32),
            dma,
            dma((ny,)), dma((ny,)), dma((nx,)), dma((nx,)), dma((nz,)), dma((nz,)),
            dma((nx,)), dma((nx,)), dma((ny,)), dma((ny,)),
        ],
        compiler_params=pltpu.CompilerParams(collective_id=1, has_side_effects=True),
        name="sum",
    )(gram)


def factor_kernel(row_total, gram_ref, rows_ref, bands_ref, factor_ref, left, right, inverse):
    size = gram_ref.shape[0]
    exact = functools.partial(
        lax.dot_general, preferred_element_type=jnp.float32, precision=lax.Precision.HIGHEST
    )
    left[...] = gram_ref[...] / row_total
    right[...] = (
        lax.broadcasted_iota(jnp.int32, (size, size), 0)
        == lax.broadcasted_iota(jnp.int32, (size, size), 1)
    ).astype(jnp.float32)
    row_at = lax.broadcasted_iota(jnp.int32, (BLOCK, BLOCK), 0)
    lane_at = lax.broadcasted_iota(jnp.int32, (BLOCK, BLOCK), 1)
    unit = (row_at == lane_at).astype(jnp.float32)
    sub = lax.broadcasted_iota(jnp.int32, (BLOCK, 1), 0)
    for k in range(size // BLOCK):
        low = k * BLOCK
        work = jnp.concatenate([left[low:low + BLOCK, low:low + BLOCK], unit], axis=1)
        for j in range(BLOCK):
            pivot = work[j:j + 1, j:j + 1]
            scale = jnp.where(sub > j, work[:, j:j + 1] * (1.0 / pivot), 0.0)
            work = work - scale * work[j:j + 1, :]
        diagonal = jnp.sum(work[:, :BLOCK] * unit, axis=1, keepdims=True)
        solver = work[:, BLOCK:] * (1.0 / jnp.sqrt(diagonal))
        upper = exact(solver, left[low:low + BLOCK, :], (((1,), (0,)), ((), ())))
        lower = exact(solver, right[low:low + BLOCK, :], (((1,), (0,)), ((), ())))
        keep = (
            lax.broadcasted_iota(jnp.int32, (BLOCK, size), 1)
            >= lax.broadcasted_iota(jnp.int32, (BLOCK, size), 0) + low
        )
        upper = jnp.where(keep, upper, 0.0)
        factor_ref[low:low + BLOCK, :] = upper
        inverse[low:low + BLOCK, :] = lower
        if low + BLOCK < size:
            edge = (low + BLOCK) // 128 * 128
            rest = upper[:, edge:]
            left[edge:, edge:] = left[edge:, edge:] - exact(rest, rest, (((0,), (0,)), ((), ())))
            right[edge:, :] = right[edge:, :] - exact(rest, lower, (((0,), (0,)), ((), ())))
    solved = split(inverse[...])
    for e in range(rows_ref.shape[0]):
        bands_ref[0, 0, e] = product(split(rows_ref[e]), solved, ((1,), (1,)))


def orthonormalise(gram, rows, row_total):
    size = gram.shape[0]
    vmem = pl.BlockSpec(memory_space=pltpu.VMEM)
    return pl.pallas_call(
        functools.partial(factor_kernel, row_total),
        out_shape=(
            jax.ShapeDtypeStruct((1, 1) + rows.shape, jnp.float32),
            jax.ShapeDtypeStruct((size, size), jnp.float32),
        ),
        in_specs=[vmem, vmem],
        out_specs=(vmem, vmem),
        scratch_shapes=[pltpu.VMEM((size, size), jnp.float32)] * 3,
        name="factor",
    )(gram, rows)


def per_device(sizes, panel, tiles, codes):
    halo = exchange_halo(panel, sizes)
    rows, gram = apply_filter(codes, panel, tiles, halo, sizes)
    summed = sum_gram(gram, sizes)
    row_total = rows.shape[0] * rows.shape[1] * sizes[0] * sizes[1] * sizes[2]
    return orthonormalise(summed, rows, float(row_total))


def solution(mesh):
    in_specs = (
        P("gx", "gy", "gz", None, None),
        P("gx", "gy", "gz", None, None, None),
        P("gx", "gy", "gz", None),
    )
    out_specs = (P("gx", "gy", "gz", None, None), P())
    sizes = tuple(mesh.shape[a] for a in ("gx", "gy", "gz"))
    return jax.shard_map(
        functools.partial(per_device, sizes),
        mesh=mesh, in_specs=in_specs, out_specs=out_specs, check_vma=False,
    )
```

time: 360 us -> 106 us (0.29)
  waiting for transfers between devices: 171 us -> 0 us
  Pallas kernels: 0 us -> 104 us
  other arithmetic: 66.5 us -> 0 us
  local copies, waits for them, and re-layouts: 42.3 us -> 1.67 us
  matrix products: 31.6 us -> 0 us
  starting transfers between devices: 15.5 us -> 0 us
  between operations: 15.9 us -> 0.69 us
  blocking collectives: 14.1 us -> 0 us
    pallas_call x0 -> x4, Pallas kernels: none -> 104 us  [the longest x1 33.6 us: exchange_halo(): pl.pallas_call(functools.partial(halo_kernel, sizes), out_shape=jax.Shape...]
    ppermute x6 -> x0, waiting for transfers between devices: 99.1 us -> none  [the longest x3 67 us: padded_2(): before = lax.ppermute(last, axis, up)]
    psum x1 -> x0, waiting for transfers between devices: 53.7 us -> none  [per_device(): gram_part = lax.psum(gram_part, ('gx', 'gy'))]
    another operation x8 -> x0, other arithmetic: 53.6 us -> none  [the longest x6 34 us: per_device(): lower = jnp.linalg.cholesky(gram)]
    dot_general x6 -> x0, matrix products: 30.3 us -> none  [the longest x4 25.7 us: per_device(): jnp.einsum('kab,kbc->ac', tiles[0, 0, element_cell], windows, precision=l...]
    gather x4 -> x0, local copies, waits for them, and re-layouts: 27.8 us -> none  [window(): lax.dynamic_slice(padded, (first, second, third, zero, zero), (1, 1, 1, p...]
    unnamed x3 -> x0, waiting for transfers between devices: 18 us -> none
    ppermute x6 -> x0, starting transfers between devices: 15.5 us -> none  [the longest x3 11.6 us: padded_2(): before = lax.ppermute(last, axis, up)]
  transfers between devices with their start and end apart: 8 -> 0, of which waited for: 8 -> 0; matrix products, arithmetic and copies ran while one was open for 2% -> 0% of each run, Pallas kernels for 0% -> 0%
where the time goes in v1:
time: 106 us
  Pallas kernels  104 us (98%)
  local copies, waits for them, and re-layouts  1.67 us (2%)
    pallas_call x1, Pallas kernels, exchange_halo(): pl.pallas_call(functools.partial(halo_kernel, sizes), out_shape=jax.Shape...  33.6 us
    pallas_call x1, Pallas kernels, orthonormalise(): pl.pallas_call(functools.partial(factor_kernel, row_total), out_shape=(ja...  29.2 us
    pallas_call x1, Pallas kernels, sum_gram(): pl.pallas_call(functools.partial(sum_kernel, sizes), out_shape=jax.ShapeD...  21.3 us
    pallas_call x1, Pallas kernels, apply_filter(): pl.pallas_call(functools.partial(filter_kernel, sizes), out_shape=(jax.Sh...  19.6 us

profile of v1, /device:TPU:0, one launch (start us, length us, event | category | flops | bytes accessed | tf_op | source)
XLA Modules:
  0.0 106.0 jit_solution(16402229697907611505)
XLA Ops:
  0.6 0.0 copy-start
  0.6 0.0 copy-start.3
  0.6 33.6 %halo.1.halo_ref = f32[3,3,6,256,256]{4,3,2,1,0:T(8,128)} custom-call(f32[1,1,4,256,256]{4,3,2,1,0:T(8,128)} %panel_ref.3), custom_call_target="tpu_custom_call" | custom-call | tf_op jit(solution)/shard_map/halo/pallas_call | solution.py:174
  34.2 0.0 copy-done
  34.2 0.0 copy-done.3
  34.2 19.6 %filter.1 = (f32[4,256,256]{2,1,0:T(8,128)S(1)}, f32[256,256]{1,0:T(8,128)S(1)}) custom-call(s32[1,1,4,10]{3,2,1,0:T(4,128)S(1)} %copy-done.3, f32[1,1,4,256,256]{4,3,2,1,0:T(8,128)S(1)} %copy-done, f32[1,1,4,10,256,256]{5,4,3,2,1,0:T(8,128)} %tiles_ref.1, f32[3,3,6,256,256]{4,3,2,1,0:T(8,128)} %halo.1.halo_ref), custom_call_target="tpu_custom_call" | custom-call | tf_op jit(solution)/shard_map/filter/pallas_call | solution.py:259
  53.9 0.0 copy-start.1
  53.9 1.0 copy-done.1
  54.8 0.0 copy-start.2
  54.8 0.7 copy-done.2
  55.5 21.3 %sum.1.gram_ref = f32[256,256]{1,0:T(8,128)} custom-call(f32[256,256]{1,0:T(8,128)} %copy-done.2), custom_call_target="tpu_custom_call" | custom-call | tf_op jit(solution)/shard_map/sum/pallas_call | solution.py:372
  76.8 29.2 %factor.1 = (f32[1,1,4,256,256]{4,3,2,1,0:T(8,128)}, f32[256,256]{1,0:T(8,128)}) custom-call(f32[256,256]{1,0:T(8,128)} %sum.1.gram_ref, f32[4,256,256]{2,1,0:T(8,128)} %copy-done.1), custom_call_target="tpu_custom_call" | custom-call | tf_op jit(solution)/shard_map/factor/pallas_call | solution.py:438
Async XLA Ops:
  0.6 33.6 %copy-start = (f32[1,1,4,256,256]{4,3,2,1,0:T(8,128)S(1)}, f32[1,1,4,256,256]{4,3,2,1,0:T(8,128)}, u32[]{:S(2)}) copy-start(f32[1,1,4,256,256]{4,3,2,1,0:T(8,128)} %panel_ref.3) | copy-start | bytes 3145732
  0.6 33.6 %copy-start.3 = (s32[1,1,4,10]{3,2,1,0:T(4,128)S(1)}, s32[1,1,4,10]{3,2,1,0:T(4,128)}, u32[]{:S(2)}) copy-start(s32[1,1,4,10]{3,2,1,0:T(4,128)} %codes_ref.1) | copy-start | bytes 484
  53.9 1.0 copy-start.1
  54.8 0.7 copy-start.2

commit v2 on v1

--- a/solution.py
+++ b/solution.py
@@ -7,8 +7,9 @@
 from jax.sharding import PartitionSpec as P
 
 MESH = pl.DeviceIdType.MESH
-PIECES = 2
-BLOCK = 32
+PIECES = 4
+BLOCK = 64
+GROUP = 16
 
 
 def split(value):
@@ -24,11 +25,15 @@
     return dot(left[0], right[0]) + (dot(left[0], right[1]) + dot(left[1], right[0]))
 
 
-def halo_kernel(sizes, panel_ref, halo_ref, x_sent, z_sent, y_sent, arrived):
+def filter_kernel(sizes, codes_ref, panel_ref, tiles_ref, rows_ref, out_ref,
+                  halo_ref, own_ref, tile_ref, high, low, tile_high, tile_low, gram_ref,
+                  own_sem, tile_sem, x_sent, z_sent, y_sent, arrived, *sum_refs):
     nx, ny, nz = sizes
     ix, iy, iz = (lax.axis_index(a) for a in ("gx", "gy", "gz"))
     depth, rows = panel_ref.shape[2], panel_ref.shape[3]
     part = rows // PIECES
+    slots, reach = tiles_ref.shape[3], depth + 2
+    empty = 9 * reach
     squared = nx == 4
     below, above = iz > 0, iz < nz - 1
     front, back = iy > 0, iy < ny - 1
@@ -39,11 +44,9 @@
         slot_a, valid_a = 2 * lax.rem(ix + 1, 2), None
         slot_b, valid_b = 2 - slot_a, (ix == 1) | (ix == 2)
         relays = (ix == 0) | (ix == 3)
-        partners_x = ((across, None), (beside, None))
     else:
         slot_a, valid_a = jnp.int32(0), ix > 0
         slot_b, valid_b = jnp.int32(2), ix < nx - 1
-        partners_x = ((ix - 1, valid_a), (ix + 1, valid_b))
 
     def when(cond, action):
         if cond is None:
@@ -55,22 +58,24 @@
         conds = [c for c in conds if c is not None]
         return functools.reduce(jnp.logical_and, conds) if conds else None
 
+    own_copy = pltpu.make_async_copy(panel_ref.at[0, 0], own_ref, own_sem)
+    own_copy.start()
+    tile_copies = [
+        pltpu.make_async_copy(tiles_ref.at[0, 0, e], tile_ref.at[e], tile_sem.at[e])
+        for e in range(depth)
+    ]
+    for tile_copy in tile_copies:
+        tile_copy.start()
+
     barrier = pltpu.get_barrier_semaphore()
-    partners = (
-        [("gx", d, c) for d, c in partners_x]
-        + [("gz", iz - 1, below), ("gz", iz + 1, above)]
-        + [("gy", iy - 1, front), ("gy", iy + 1, back)]
-    )
-    total = jnp.int32(0)
-    for axis, device, cond in partners:
-        when(
-            cond,
-            lambda axis=axis, device=device: pl.semaphore_signal(
-                barrier, inc=1, device_id={axis: device}, device_id_type=MESH
-            ),
-        )
-        total = total + (1 if cond is None else cond.astype(jnp.int32))
-    pl.semaphore_wait(barrier, total)
+    peers = {
+        axis: [lax.rem(at + d, n) for d in range(1, n)]
+        for axis, at, n in (("gx", ix, nx), ("gy", iy, ny), ("gz", iz, nz))
+    }
+    for axis, group in peers.items():
+        for peer in group:
+            pl.semaphore_signal(barrier, inc=1, device_id={axis: peer}, device_id_type=MESH)
+    pl.semaphore_wait(barrier, nx + ny + nz - 3)
 
     sends = []
 
@@ -147,153 +152,117 @@
                 wait(ok, a, 1, slot, c)
                 send_y(ok, cell(a, 1, slot, c), a, slot, c)
 
+    def place(a, b, z):
+        return (a * 3 + b) * reach + z
+
+    def keep(cond, a, b, z):
+        def act():
+            high[place(a, b, z)], low[place(a, b, z)] = split(halo_ref[a, b, z])
+
+        when(cond, act)
+
+    def take_y(cond, a, z):
+        edge = below if z == 0 else above if z == depth + 1 else None
+        for b, side in ((0, front), (2, back)):
+            ok = both(cond, edge, side)
+            for c in range(PIECES):
+                wait(ok, a, b, z, c)
+            keep(ok, a, b, z)
+
+    def keep_z(cond, a):
+        keep(both(cond, below), a, 1, 0)
+        keep(both(cond, above), a, 1, depth + 1)
+
+    def take_y_z(cond, a):
+        take_y(cond, a, 0)
+        take_y(cond, a, depth + 1)
+
     steps = [(k, c) for k in order for c in range(PIECES)]
-    for at in range(len(steps) + 1):
-        if at < len(steps):
+    last = len(steps)
+    work = [[] for _ in range(last + 1)]
+
+    def later(step, action, *args):
+        work[min(step, last)].append((action, args))
+
+    def keep_own(z):
+        if z == 0:
+            own_copy.wait()
+        high[place(1, 1, z + 1)], low[place(1, 1, z + 1)] = split(own_ref[z])
+
+    def keep_tiles(e, begin, end):
+        if begin == 0:
+            tile_copies[e].wait()
+
+        def body(s, carry):
+            tile_high[e * slots + s], tile_low[e * slots + s] = split(tile_ref[e, s])
+            return carry
+
+        lax.fori_loop(begin, end, body, 0)
+
+    cuts = list(range(0, slots, 3)) + [slots]
+    chunks = [(e, p, q) for e in range(depth) for p, q in zip(cuts[:-1], cuts[1:])]
+    for at, chunk in enumerate(chunks):
+        later(1 + at * max(last - 3, 1) // len(chunks), keep_tiles, *chunk)
+    for at, z in enumerate(order):
+        later(at, keep_own, at)
+        later((at + 2) * PIECES // 2, take_y, None, 1, z + 1)
+        later((at + 1) * PIECES - 1, keep, valid_a, slot_a, 1, z + 1)
+        later((at + 1) * PIECES, keep, valid_b, slot_b, 1, z + 1)
+        later((at + 1) * PIECES + 2, take_y, valid_a, slot_a, z + 1)
+        later((at + 1) * PIECES + 3, take_y, valid_b, slot_b, z + 1)
+    half = last // 2
+    high[empty] = jnp.zeros(high.shape[1:], high.dtype)
+    low[empty] = jnp.zeros(low.shape[1:], low.dtype)
+    for at in range(last + 1):
+        if at < last:
             arrive(valid_a, slot_a, *steps[at], relay=True)
         if at >= 1:
             arrive(valid_b, slot_b, *steps[at - 1])
-        if at == len(steps) // 2:
+        if at == half:
             arrive_z(None, 1)
-        if at == len(steps) - 1:
+            keep_z(None, 1)
+            later(half + 3, take_y_z, None, 1)
+        if at == last - 2:
             arrive_z(valid_a, slot_a)
-    arrive_z(valid_b, slot_b)
-
-    for b, side in ((0, front), (2, back)):
-        for a, cond in ((1, None), (slot_a, valid_a), (slot_b, valid_b)):
-            for z in range(depth + 2):
-                edge = below if z == 0 else above if z == depth + 1 else None
-                for c in range(PIECES):
-                    wait(both(cond, edge, side), a, b, z, c)
-    for cond, source, sem in sends:
-        when(cond, lambda source=source, sem=sem: pltpu.make_async_copy(source, source, sem).wait())
-
-
-def exchange_halo(panel, sizes):
-    depth, rows, width = panel.shape[2:]
-    return pl.pallas_call(
-        functools.partial(halo_kernel, sizes),
-        out_shape=jax.ShapeDtypeStruct((3, 3, depth + 2, rows, width), panel.dtype),
-        in_specs=[pl.BlockSpec(memory_space=pl.ANY)],
-        out_specs=pl.BlockSpec(memory_space=pl.ANY),
-        scratch_shapes=[
-            pltpu.SemaphoreType.DMA((2, depth, PIECES)),
-            pltpu.SemaphoreType.DMA((2, 3, PIECES)),
-            pltpu.SemaphoreType.DMA((2, 3, depth + 2, PIECES)),
-            pltpu.SemaphoreType.DMA((3, 3, depth + 2, PIECES)),
-        ],
-        compiler_params=pltpu.CompilerParams(collective_id=0, has_side_effects=True),
-        name="halo",
-    )(panel)
-
-
-def filter_kernel(sizes, codes_ref, panel_ref, tiles_ref, halo_ref, rows_ref, gram_ref,
-                  tile_buf, window_buf, own_buf, tile_sem, window_sem, own_sem):
-    nx, ny, nz = sizes
-    ix, iy, iz = (lax.axis_index(a) for a in ("gx", "gy", "gz"))
-    depth, slots = tiles_ref.shape[2], tiles_ref.shape[3]
-    own = pltpu.make_async_copy(panel_ref.at[0, 0], own_buf, own_sem)
-    own.start()
-
-    def place(e, s):
-        code = codes_ref[0, 0, e, s]
-        a = code // 9
-        b = lax.rem(code // 3, 3)
-        z = e + lax.rem(code, 3)
-        x_at, y_at, z_at = ix + a - 1, iy + b - 1, iz * depth + z - 1
-        inside = ((x_at >= 0) & (x_at < nx) & (y_at >= 0) & (y_at < ny)
-                  & (z_at >= 0) & (z_at < nz * depth))
-        local = (a == 1) & (b == 1) & (z >= 1) & (z <= depth)
-        return a, b, z, inside, local
+            keep_z(valid_a, slot_a)
+            later(last, take_y_z, valid_a, slot_a)
+        if at == last - 1:
+            arrive_z(valid_b, slot_b)
+            keep_z(valid_b, slot_b)
+            later(last, take_y_z, valid_b, slot_b)
+        for action, args in work[at]:
+            action(*args)
 
     for e in range(depth):
-        pltpu.make_async_copy(tiles_ref.at[0, 0, e], tile_buf.at[e], tile_sem.at[e]).start()
-
-        def fetch(s, carry, e=e):
-            a, b, z, inside, local = place(e, s)
-            target, sem = window_buf.at[e, s], window_sem.at[e, s]
-
-            @pl.when(inside & local)
-            def _():
-                pltpu.make_async_copy(panel_ref.at[0, 0, z - 1], target, sem).start()
-
-            @pl.when(inside & jnp.logical_not(local))
-            def _():
-                pltpu.make_async_copy(halo_ref.at[a, b, z], target, sem).start()
-
-            @pl.when(jnp.logical_not(inside))
-            def _():
-                window_buf[e, s] = jnp.zeros(window_buf.shape[2:], window_buf.dtype)
-
-            return carry
-
-        lax.fori_loop(0, slots, fetch, 0)
-    own.wait()
-    for e in range(depth):
-        pltpu.make_async_copy(tiles_ref.at[0, 0, e], tile_buf.at[e], tile_sem.at[e]).wait()
-
         def apply(s, total, e=e):
-            inside = place(e, s)[3]
-
-            @pl.when(inside)
-            def _():
-                pltpu.make_async_copy(
-                    window_buf.at[e, s], window_buf.at[e, s], window_sem.at[e, s]
-                ).wait()
-
+            code = codes_ref[0, 0, e, s]
+            a, b, z = code // 9, lax.rem(code // 3, 3), e + lax.rem(code, 3)
+            x_at, y_at, z_at = ix + a - 1, iy + b - 1, iz * depth + z - 1
+            inside = ((x_at >= 0) & (x_at < nx) & (y_at >= 0) & (y_at < ny)
+                      & (z_at >= 0) & (z_at < nz * depth))
+            at = jnp.where(inside, place(a, b, z), empty)
+            tile = e * slots + s
             return total + product(
-                split(tile_buf[e, s]), split(window_buf[e, s]), ((1,), (0,))
+                (tile_high[tile], tile_low[tile]), (high[at], low[at]), ((1,), (0,))
             )
 
-        filtered = lax.fori_loop(0, slots, apply, -0.5 * own_buf[e], unroll=2)
+        filtered = lax.fori_loop(0, slots, apply, -0.5 * own_ref[e], unroll=2)
         rows_ref[e] = filtered
         pieces = split(filtered)
         term = product(pieces, pieces, ((0,), (0,)))
         gram_ref[...] = term if e == 0 else gram_ref[...] + term
-
-
-def apply_filter(codes, panel, tiles, halo, sizes):
-    depth, slots, rows, width = tiles.shape[2], tiles.shape[3], panel.shape[3], panel.shape[4]
-    hbm = pl.BlockSpec(memory_space=pl.ANY)
-    vmem = pl.BlockSpec(memory_space=pltpu.VMEM)
-    return pl.pallas_call(
-        functools.partial(filter_kernel, sizes),
-        out_shape=(
-            jax.ShapeDtypeStruct((depth, rows, width), jnp.float32),
-            jax.ShapeDtypeStruct((width, width), jnp.float32),
-        ),
-        in_specs=[pl.BlockSpec(memory_space=pltpu.SMEM), hbm, hbm, hbm],
-        out_specs=(vmem, vmem),
-        scratch_shapes=[
-            pltpu.VMEM((depth, slots, rows, rows), jnp.float32),
-            pltpu.VMEM((depth, slots, rows, width), jnp.float32),
-            pltpu.VMEM((depth, rows, width), jnp.float32),
-            pltpu.SemaphoreType.DMA((depth,)),
-            pltpu.SemaphoreType.DMA((depth, slots)),
-            pltpu.SemaphoreType.DMA,
-        ],
-        compiler_params=pltpu.CompilerParams(vmem_limit_bytes=48 << 20),
-        name="filter",
-    )(codes, panel, tiles, halo)
-
-
-def sum_kernel(sizes, gram_ref, out_ref, own, from_y, part_y, from_x, from_z, full,
-               local_sem, y_send, y_recv, x_send, x_recv, z_send, z_recv,
+    sum_over_mesh(sizes, peers, gram_ref, out_ref, *sum_refs)
+    for cond, source, sem in sends:
+        when(cond, lambda source=source, sem=sem: pltpu.make_async_copy(source, source, sem).wait())
+
+
+def sum_over_mesh(sizes, peers, gram_ref, out_ref, from_y, part_y, from_x, from_z, full,
+                  y_send, y_recv, x_send, x_recv, z_send, z_recv,
                gx_send, gx_recv, gy_send, gy_recv):
     nx, ny, nz = sizes
     ix, iy, iz = (lax.axis_index(a) for a in ("gx", "gy", "gz"))
     rows_y = gram_ref.shape[0] // ny
     rows_x = rows_y // nx
-    barrier = pltpu.get_barrier_semaphore()
-    peers = {
-        axis: [lax.rem(at + d, n) for d in range(1, n)]
-        for axis, at, n in (("gx", ix, nx), ("gy", iy, ny), ("gz", iz, nz))
-    }
-    for axis, group in peers.items():
-        for peer in group:
-            pl.semaphore_signal(barrier, inc=1, device_id={axis: peer}, device_id_type=MESH)
-    pl.semaphore_wait(barrier, nx + ny + nz - 3)
-
     def copy(source, target, send_sem, recv_sem, axis, peer):
         remote = pltpu.make_async_remote_copy(
             src_ref=source, dst_ref=target, send_sem=send_sem, recv_sem=recv_sem,
@@ -362,32 +331,52 @@
     out_ref[...] = full[...]
 
 
-def sum_gram(gram, sizes):
+def filter_and_gram(codes, panel, tiles, sizes):
     nx, ny, nz = sizes
-    size = gram.shape[0]
-    rows_y = size // ny
+    depth, slots, rows, width = tiles.shape[2], tiles.shape[3], panel.shape[3], panel.shape[4]
+    reach = depth + 2
+    rows_y = width // ny
     rows_x = rows_y // nx
+    hbm = pl.BlockSpec(memory_space=pl.ANY)
     vmem = pl.BlockSpec(memory_space=pltpu.VMEM)
     dma = pltpu.SemaphoreType.DMA
+    half = jnp.bfloat16
     return pl.pallas_call(
-        functools.partial(sum_kernel, sizes),
-        out_shape=jax.ShapeDtypeStruct(gram.shape, gram.dtype),
-        in_specs=[vmem],
-        out_specs=vmem,
+        functools.partial(filter_kernel, sizes),
+        out_shape=(
+            jax.ShapeDtypeStruct((depth, rows, width), jnp.float32),
+            jax.ShapeDtypeStruct((width, width), jnp.float32),
+        ),
+        in_specs=[pl.BlockSpec(memory_space=pltpu.SMEM), hbm, hbm],
+        out_specs=(vmem, vmem),
         scratch_shapes=[
-            pltpu.VMEM((8, 128), jnp.float32),
-            pltpu.VMEM((max(ny - 1, 1), rows_y, size), jnp.float32),
-            pltpu.VMEM((rows_y, size), jnp.float32),
-            pltpu.VMEM((max(nx - 1, 1), rows_x, size), jnp.float32),
-            pltpu.VMEM((nz, rows_x, size), jnp.float32),
-            pltpu.VMEM((size, size), jnp.float32),
+            pltpu.VMEM((3, 3, reach, rows, width), jnp.float32),
+            pltpu.VMEM((depth, rows, width), jnp.float32),
+            pltpu.VMEM((depth, slots, rows, rows), jnp.float32),
+            pltpu.VMEM((9 * reach + 1, rows, width), half),
+            pltpu.VMEM((9 * reach + 1, rows, width), half),
+            pltpu.VMEM((depth * slots, rows, rows), half),
+            pltpu.VMEM((depth * slots, rows, rows), half),
+            pltpu.VMEM((width, width), jnp.float32),
             dma,
+            dma((depth,)),
+            dma((2, depth, PIECES)),
+            dma((2, 3, PIECES)),
+            dma((2, 3, reach, PIECES)),
+            dma((3, 3, reach, PIECES)),
+            pltpu.VMEM((max(ny - 1, 1), rows_y, width), jnp.float32),
+            pltpu.VMEM((rows_y, width), jnp.float32),
+            pltpu.VMEM((max(nx - 1, 1), rows_x, width), jnp.float32),
+            pltpu.VMEM((nz, rows_x, width), jnp.float32),
+            pltpu.VMEM((width, width), jnp.float32),
             dma((ny,)), dma((ny,)), dma((nx,)), dma((nx,)), dma((nz,)), dma((nz,)),
             dma((nx,)), dma((nx,)), dma((ny,)), dma((ny,)),
         ],
-        compiler_params=pltpu.CompilerParams(collective_id=1, has_side_effects=True),
-        name="sum",
-    )(gram)
+        compiler_params=pltpu.CompilerParams(
+            collective_id=0, has_side_effects=True, vmem_limit_bytes=61 << 20
+        ),
+        name="filter",
+    )(codes, panel, tiles)
 
 
 def factor_kernel(row_total, gram_ref, rows_ref, bands_ref, factor_ref, left, right, inverse):
@@ -403,14 +392,22 @@
     row_at = lax.broadcasted_iota(jnp.int32, (BLOCK, BLOCK), 0)
     lane_at = lax.broadcasted_iota(jnp.int32, (BLOCK, BLOCK), 1)
     unit = (row_at == lane_at).astype(jnp.float32)
-    sub = lax.broadcasted_iota(jnp.int32, (BLOCK, 1), 0)
+    sub = lax.broadcasted_iota(jnp.int32, (BLOCK, 2 * BLOCK), 0)
     for k in range(size // BLOCK):
         low = k * BLOCK
         work = jnp.concatenate([left[low:low + BLOCK, low:low + BLOCK], unit], axis=1)
-        for j in range(BLOCK):
-            pivot = work[j:j + 1, j:j + 1]
-            scale = jnp.where(sub > j, work[:, j:j + 1] * (1.0 / pivot), 0.0)
-            work = work - scale * work[j:j + 1, :]
+        for start in range(0, BLOCK, GROUP):
+            columns = [
+                jnp.broadcast_to(work[:, j:j + 1], (BLOCK, 2 * BLOCK))
+                for j in range(start, start + GROUP)
+            ]
+            for at in range(GROUP):
+                j = start + at
+                inverted = 1.0 / columns[at][j:j + 1, :]
+                scale = jnp.where(sub > j, columns[at] * inverted, 0.0)
+                for later in range(at + 1, GROUP):
+                    columns[later] = columns[later] - scale * columns[later][j:j + 1, :]
+                work = work - scale * work[j:j + 1, :]
         diagonal = jnp.sum(work[:, :BLOCK] * unit, axis=1, keepdims=True)
         solver = work[:, BLOCK:] * (1.0 / jnp.sqrt(diagonal))
         upper = exact(solver, left[low:low + BLOCK, :], (((1,), (0,)), ((), ())))
@@ -449,9 +446,7 @@
 
 
 def per_device(sizes, panel, tiles, codes):
-    halo = exchange_halo(panel, sizes)
-    rows, gram = apply_filter(codes, panel, tiles, halo, sizes)
-    summed = sum_gram(gram, sizes)
+    rows, summed = filter_and_gram(codes, panel, tiles, sizes)
     row_total = rows.shape[0] * rows.shape[1] * sizes[0] * sizes[1] * sizes[2]
     return orthonormalise(summed, rows, float(row_total))
 

time: 106 us -> 75.9 us (0.72)
  Pallas kernels: 104 us -> 75.1 us
  local copies, waits for them, and re-layouts: 1.67 us -> 0 us
    pallas_call x1, Pallas kernels: 29.2 us -> 11.7 us  [orthonormalise(): pl.pallas_call(functools.partial(factor_kernel, row_total), out_shape=(ja...]
    pallas_call x3 -> x1, Pallas kernels: 74.4 us -> 63.4 us  [filter_and_gram(): pl.pallas_call(functools.partial(filter_kernel, sizes), out_shape=(jax.Sh...]
    unnamed x8 -> x0, local copies, waits for them, and re-layouts: 1.67 us -> none
where the time goes in v2:
time: 75.9 us; the launch traced here: 75.7 us
  Pallas kernels  75.1 us (99%)
    pallas_call x1, Pallas kernels, filter_and_gram(): pl.pallas_call(functools.partial(filter_kernel, sizes), out_shape=(jax.Sh...  63.4 us
    pallas_call x1, Pallas kernels, orthonormalise(): pl.pallas_call(functools.partial(factor_kernel, row_total), out_shape=(ja...  11.7 us

profile of v2, /device:TPU:0, one launch (start us, length us, event | category | flops | bytes accessed | tf_op | source)
XLA Modules:
  0.0 75.7 jit_solution(16612102970391345167)
XLA Ops:
  0.6 63.4 %filter.1 = (f32[4,256,256]{2,1,0:T(8,128)}, f32[256,256]{1,0:T(8,128)}) custom-call(s32[1,1,4,10]{3,2,1,0:T(4,128)} %codes_ref.1, f32[1,1,4,256,256]{4,3,2,1,0:T(8,128)} %panel_ref.1, f32[1,1,4,10,256,256]{5,4,3,2,1,0:T(8,128)} %tiles_ref.1), custom_call_target="tpu_custom_call" | custom-call | tf_op jit(solution)/shard_map/filter/pallas_call | solution.py:344
  64.0 11.7 %factor.1 = (f32[1,1,4,256,256]{4,3,2,1,0:T(8,128)}, f32[256,256]{1,0:T(8,128)}) custom-call(f32[256,256]{1,0:T(8,128)} %get-tuple-element.4.gram_ref, f32[4,256,256]{2,1,0:T(8,128)} %get-tuple-element.5.rows_ref), custom_call_target="tpu_custom_call" | custom-call | tf_op jit(solution)/shard_map/factor/pallas_call | solution.py:435

commit v3 on v2

--- a/solution.py
+++ b/solution.py
@@ -233,36 +233,64 @@
         for action, args in work[at]:
             action(*args)
 
+    highs, lows = [], []
     for e in range(depth):
-        def apply(s, total, e=e):
-            code = codes_ref[0, 0, e, s]
+        left, right = [], []
+        for slot in range(slots):
+            code = codes_ref[0, 0, e, slot]
             a, b, z = code // 9, lax.rem(code // 3, 3), e + lax.rem(code, 3)
             x_at, y_at, z_at = ix + a - 1, iy + b - 1, iz * depth + z - 1
             inside = ((x_at >= 0) & (x_at < nx) & (y_at >= 0) & (y_at < ny)
                       & (z_at >= 0) & (z_at < nz * depth))
             at = jnp.where(inside, place(a, b, z), empty)
-            tile = e * slots + s
-            return total + product(
-                (tile_high[tile], tile_low[tile]), (high[at], low[at]), ((1,), (0,))
-            )
-
-        filtered = lax.fori_loop(0, slots, apply, -0.5 * own_ref[e], unroll=2)
+            tile = e * slots + slot
+            left += [tile_high[tile], tile_low[tile], tile_high[tile]]
+            right += [high[at], high[at], low[at]]
+        filtered = -0.5 * own_ref[e] + lax.dot_general(
+            jnp.concatenate(left, axis=1), jnp.concatenate(right, axis=0),
+            (((1,), (0,)), ((), ())), preferred_element_type=jnp.float32,
+        )
         rows_ref[e] = filtered
         pieces = split(filtered)
-        term = product(pieces, pieces, ((0,), (0,)))
-        gram_ref[...] = term if e == 0 else gram_ref[...] + term
+        highs.append(pieces[0])
+        lows.append(pieces[1])
+    tall = functools.partial(
+        lax.dot_general, dimension_numbers=(((0,), (0,)), ((), ())),
+        preferred_element_type=jnp.float32,
+    )
+    whole_high = jnp.concatenate(highs, axis=0)
+    mixed = tall(whole_high, jnp.concatenate(lows, axis=0))
+    gram = tall(whole_high, whole_high) + mixed + mixed.T
+    for part_at, (rows_at, lanes_at) in enumerate(gram_parts(sizes, gram.shape[0])):
+        gram_ref[part_at] = gram[rows_at:rows_at + gram_ref.shape[1], lanes_at:lanes_at + 128]
     sum_over_mesh(sizes, peers, gram_ref, out_ref, *sum_refs)
     for cond, source, sem in sends:
         when(cond, lambda source=source, sem=sem: pltpu.make_async_copy(source, source, sem).wait())
 
 
+def gram_parts(sizes, size):
+    half = size // 2
+    folded = half % 128 == 0 and half % (sizes[0] * sizes[1] * 8) == 0
+    lanes = range(0, size, 128)
+    if not folded:
+        return [(0, lane) for lane in lanes]
+    return [(0, lane) for lane in lanes] + [(half, lane) for lane in lanes if lane >= half]
+
+
+def part_rows(sizes, size):
+    return size // 2 if gram_parts(sizes, size)[-1][0] else size
+
+
 def sum_over_mesh(sizes, peers, gram_ref, out_ref, from_y, part_y, from_x, from_z, full,
                   y_send, y_recv, x_send, x_recv, z_send, z_recv,
-               gx_send, gx_recv, gy_send, gy_recv):
+                  gx_send, gx_recv, gy_send, gy_recv):
     nx, ny, nz = sizes
     ix, iy, iz = (lax.axis_index(a) for a in ("gx", "gy", "gz"))
-    rows_y = gram_ref.shape[0] // ny
+    count, rows = gram_ref.shape[:2]
+    rows_y = rows // ny
     rows_x = rows_y // nx
+    mine = iy * nx + ix
+
     def copy(source, target, send_sem, recv_sem, axis, peer):
         remote = pltpu.make_async_remote_copy(
             src_ref=source, dst_ref=target, send_sem=send_sem, recv_sem=recv_sem,
@@ -271,71 +299,91 @@
         remote.start()
         return remote
 
-    def finish(copies):
-        for remote in copies:
+    def window(at, size):
+        return pl.ds(pl.multiple_of(at * size, size), size)
+
+    def landed(started, group, ref_of, sems, p):
+        for remote in started:
+            remote.wait_send()
+        for peer in group:
+            ref = ref_of(peer)
+            pltpu.make_async_copy(ref, ref, sems.at[peer, p]).wait()
+
+    def start_y(p, started):
+        return [
+            copy(gram_ref.at[p, window(peer, rows_y)], from_y.at[d, p],
+                 y_send.at[d, p], y_recv.at[d, p], "gy", peer)
+            for d, peer in enumerate(peers["gy"])
+        ]
+
+    def start_x(p, started):
+        for remote in started:
             remote.wait()
-
-    def block(ref, at, count):
-        return ref.at[pl.ds(pl.multiple_of(at * count, count), count)]
-
-    finish([
-        copy(block(gram_ref, peer, rows_y), from_y.at[d], y_send.at[d], y_recv.at[d], "gy", peer)
-        for d, peer in enumerate(peers["gy"])
-    ])
-    total = gram_ref[pl.ds(pl.multiple_of(iy * rows_y, rows_y), rows_y), :]
-    for d in range(ny - 1):
-        total = total + from_y[d]
-    part_y[...] = total
-    finish([
-        copy(block(part_y, peer, rows_x), from_x.at[d], x_send.at[d], x_recv.at[d], "gx", peer)
-        for d, peer in enumerate(peers["gx"])
-    ])
-    total = part_y[pl.ds(pl.multiple_of(ix * rows_x, rows_x), rows_x), :]
-    for d in range(nx - 1):
-        total = total + from_x[d]
-    from_z[pl.ds(iz, 1)] = total[None]
-    started = [
-        copy(from_z.at[iz], from_z.at[iz], z_send.at[d], z_recv.at[iz], "gz", peer)
-        for d, peer in enumerate(peers["gz"])
-    ]
-    for remote in started:
-        remote.wait_send()
-    for peer in peers["gz"]:
-        ref = from_z.at[peer]
-        pltpu.make_async_copy(ref, ref, z_recv.at[peer]).wait()
-    total = from_z[0]
-    for d in range(1, nz):
-        total = total + from_z[d]
-    mine = iy * nx + ix
-    full[pl.ds(pl.multiple_of(mine * rows_x, rows_x), rows_x), :] = total
-    started = [
-        copy(block(full, mine, rows_x), block(full, mine, rows_x), gx_send.at[d], gx_recv.at[ix],
-             "gx", peer)
-        for d, peer in enumerate(peers["gx"])
-    ]
-    for remote in started:
-        remote.wait_send()
-    for peer in peers["gx"]:
-        ref = block(full, iy * nx + peer, rows_x)
-        pltpu.make_async_copy(ref, ref, gx_recv.at[peer]).wait()
-    started = [
-        copy(block(full, iy, rows_y), block(full, iy, rows_y), gy_send.at[d], gy_recv.at[iy],
-             "gy", peer)
-        for d, peer in enumerate(peers["gy"])
-    ]
-    for remote in started:
-        remote.wait_send()
-    for peer in peers["gy"]:
-        ref = block(full, peer, rows_y)
-        pltpu.make_async_copy(ref, ref, gy_recv.at[peer]).wait()
-    out_ref[...] = full[...]
+        total = gram_ref[p, window(iy, rows_y), :]
+        for d in range(ny - 1):
+            total = total + from_y[d, p]
+        part_y[p] = total
+        return [
+            copy(part_y.at[p, window(peer, rows_x)], from_x.at[d, p],
+                 x_send.at[d, p], x_recv.at[d, p], "gx", peer)
+            for d, peer in enumerate(peers["gx"])
+        ]
+
+    def start_z(p, started):
+        for remote in started:
+            remote.wait()
+        total = part_y[p, window(ix, rows_x), :]
+        for d in range(nx - 1):
+            total = total + from_x[d, p]
+        from_z[iz, p] = total
+        return [
+            copy(from_z.at[iz, p], from_z.at[iz, p], z_send.at[d, p], z_recv.at[iz, p],
+                 "gz", peer)
+            for d, peer in enumerate(peers["gz"])
+        ]
+
+    def gather_x(p, started):
+        landed(started, peers["gz"], lambda peer: from_z.at[peer, p], z_recv, p)
+        total = from_z[0, p]
+        for d in range(1, nz):
+            total = total + from_z[d, p]
+        full[p, window(mine, rows_x), :] = total
+        ref = full.at[p, window(mine, rows_x)]
+        return [
+            copy(ref, ref, gx_send.at[d, p], gx_recv.at[ix, p], "gx", peer)
+            for d, peer in enumerate(peers["gx"])
+        ]
+
+    def gather_y(p, started):
+        landed(started, peers["gx"],
+               lambda peer: full.at[p, window(iy * nx + peer, rows_x)], gx_recv, p)
+        ref = full.at[p, window(iy, rows_y)]
+        return [
+            copy(ref, ref, gy_send.at[d, p], gy_recv.at[iy, p], "gy", peer)
+            for d, peer in enumerate(peers["gy"])
+        ]
+
+    started = [None] * count
+    for phase in (start_y, start_x, start_z, gather_x, gather_y):
+        for p in range(count):
+            started[p] = phase(p, started[p])
+    size = out_ref.shape[0]
+    corners = gram_parts(sizes, size)
+    if rows < size:
+        out_ref[rows:, :rows] = jnp.zeros((size - rows, rows), out_ref.dtype)
+    for p in range(count):
+        landed(started[p], peers["gy"], lambda peer: full.at[p, window(peer, rows_y)], gy_recv, p)
+        row, lane = corners[p]
+        out_ref[row:row + rows, lane:lane + 128] = full[p]
 
 
 def filter_and_gram(codes, panel, tiles, sizes):
     nx, ny, nz = sizes
     depth, slots, rows, width = tiles.shape[2], tiles.shape[3], panel.shape[3], panel.shape[4]
     reach = depth + 2
-    rows_y = width // ny
+    parts = len(gram_parts(sizes, width))
+    gram_rows = part_rows(sizes, width)
+    rows_y = gram_rows // ny
     rows_x = rows_y // nx
     hbm = pl.BlockSpec(memory_space=pl.ANY)
     vmem = pl.BlockSpec(memory_space=pltpu.VMEM)
@@ -357,20 +405,19 @@
             pltpu.VMEM((9 * reach + 1, rows, width), half),
             pltpu.VMEM((depth * slots, rows, rows), half),
             pltpu.VMEM((depth * slots, rows, rows), half),
-            pltpu.VMEM((width, width), jnp.float32),
+            pltpu.VMEM((parts, gram_rows, 128), jnp.float32),
             dma,
             dma((depth,)),
             dma((2, depth, PIECES)),
             dma((2, 3, PIECES)),
             dma((2, 3, reach, PIECES)),
             dma((3, 3, reach, PIECES)),
-            pltpu.VMEM((max(ny - 1, 1), rows_y, width), jnp.float32),
-            pltpu.VMEM((rows_y, width), jnp.float32),
-            pltpu.VMEM((max(nx - 1, 1), rows_x, width), jnp.float32),
-            pltpu.VMEM((nz, rows_x, width), jnp.float32),
-            pltpu.VMEM((width, width), jnp.float32),
-            dma((ny,)), dma((ny,)), dma((nx,)), dma((nx,)), dma((nz,)), dma((nz,)),
-            dma((nx,)), dma((nx,)), dma((ny,)), dma((ny,)),
+            pltpu.VMEM((max(ny - 1, 1), parts, rows_y, 128), jnp.float32),
+            pltpu.VMEM((parts, rows_y, 128), jnp.float32),
+            pltpu.VMEM((max(nx - 1, 1), parts, rows_x, 128), jnp.float32),
+            pltpu.VMEM((nz, parts, rows_x, 128), jnp.float32),
+            pltpu.VMEM((parts, gram_rows, 128), jnp.float32),
+            *[dma((n, parts)) for n in (ny, ny, nx, nx, nz, nz, nx, nx, ny, ny)],
         ],
         compiler_params=pltpu.CompilerParams(
             collective_id=0, has_side_effects=True, vmem_limit_bytes=61 << 20

time: 75.9 us -> 69.9 us (0.921)
  Pallas kernels: 75.1 us -> 69.1 us
    pallas_call x1, Pallas kernels: 63.4 us -> 57.4 us  [filter_and_gram(): pl.pallas_call(functools.partial(filter_kernel, sizes), out_shape=(jax.Sh...]
where the time goes in v3:
time: 69.9 us; the launch traced here: 69.7 us
  Pallas kernels  69.1 us (99%)
    pallas_call x1, Pallas kernels, filter_and_gram(): pl.pallas_call(functools.partial(filter_kernel, sizes), out_shape=(jax.Sh...  57.4 us
    pallas_call x1, Pallas kernels, orthonormalise(): pl.pallas_call(functools.partial(factor_kernel, row_total), out_shape=(ja...  11.7 us

profile of v3, /device:TPU:0, one launch (start us, length us, event | category | flops | bytes accessed | tf_op | source)
XLA Modules:
  0.0 69.7 jit_solution(8246614248515471343)
XLA Ops:
  0.6 57.4 %filter.1 = (f32[4,256,256]{2,1,0:T(8,128)}, f32[256,256]{1,0:T(8,128)}) custom-call(s32[1,1,4,10]{3,2,1,0:T(4,128)} %codes_ref.1, f32[1,1,4,256,256]{4,3,2,1,0:T(8,128)} %panel_ref.1, f32[1,1,4,10,256,256]{5,4,3,2,1,0:T(8,128)} %tiles_ref.1), custom_call_target="tpu_custom_call" | custom-call | tf_op jit(solution)/shard_map/filter/pallas_call | solution.py:392
  58.0 11.7 %factor.1 = (f32[1,1,4,256,256]{4,3,2,1,0:T(8,128)}, f32[256,256]{1,0:T(8,128)}) custom-call(f32[256,256]{1,0:T(8,128)} %get-tuple-element.4.gram_ref, f32[4,256,256]{2,1,0:T(8,128)} %get-tuple-element.5.rows_ref), custom_call_target="tpu_custom_call" | custom-call | tf_op jit(solution)/shard_map/factor/pallas_call | solution.py:482
